TPU v7x, 128 devices: a whole 4x4x4 slice. The times are simulated.
128 devices in a mesh: orow: 16 (over z, x), ocol: 8 (over y, core).
Axes of the slice: x: 4, y: 4, z: 4, core: 2. Of those that a mesh axis runs over, the one named last changes fastest.
Arguments:
- integrals: bfloat16 [2304, 32, 384], P('ocol', 'orow'), may hold values from -0.29882812 to 0.29882812
- occ_count: int32 [16], replicated, may hold values from 1 to 2
- occ_energy: float32 [32], replicated, may hold values from -2 to -0.5
- vir_energy: float32 [384], replicated, may hold values from 0.3 to 2.5
- task_iblock: int32 [64, 1], replicated, may hold values from 0 to 15; in each aligned block of 64 rows (0 to 63, 64 to 127, ...) at most 8 rows name the same one
- task_jblock: int32 [64], replicated, may hold values from 0 to 15
Outputs:
- gamma_out: float32 [2304, 32, 384], P('ocol', 'orow')
- density: float32 [384, 384], replicated
Inputs may be any that keep to these rules, and one draw needn't show every extreme that they name: `task_iblock`: no first block is named by more than 8 tasks, and some first block by exactly 8.
All inputs are finite; a program needn't handle non-finite values.
Results may differ from a plain program's by a relative error of at most 0.0019.
Values may be sent and summed in bfloat16 or wider, within the bound.
No kernel may reach another device: no remote copies, remote signals or barrier semaphores. Data moves between devices by JAX's collectives and lax.ppermute only.
A program may use at most 128 MiB of HBM per device.

v0:
```python
import jax
import jax.numpy as jnp
from jax import lax
from jax.sharding import Mesh
from jax.sharding import PartitionSpec as P

OROW = ("orow_0", "orow_1")
OCOL = ("ocol_0", "ocol_1")
OROW_OCOL = ("orow_0", "orow_1", "ocol_0", "ocol_1")


def rows_for(lines, length):
    spare = -lines.shape[0] % length
    if not spare:
        return lines
    return jnp.concatenate([lines, jnp.zeros((spare, *lines.shape[1:]), lines.dtype)])


def sum_in_order(pieces, axes, turns):
    lengths = [lax.axis_size(a) for a in axes]
    pieces = pieces.reshape(*lengths, *pieces.shape[1:])
    pieces = pieces.transpose(*turns, *range(len(axes), pieces.ndim))
    pieces = pieces.reshape(-1, *pieces.shape[len(axes) :])
    for k in turns:
        pieces = lax.psum_scatter(pieces, axes[k], scatter_dimension=0, tiled=True)
    return pieces[0]


def gather_in_order(x, axes, turns):
    pieces = x
    for k in turns:
        pieces = lax.all_gather(pieces, axes[k])
    done = turns[::-1]
    back = [done.index(k) for k in range(len(axes))]
    pieces = pieces.transpose(*back, *range(len(axes), pieces.ndim))
    return pieces.reshape(-1, *x.shape)


def total_of(x, axes, turns):
    length, lines = (lax.axis_size(axes), x.reshape(-1, *x.shape[1:][-1:]))
    pieces = rows_for(lines, length).reshape(length, -1, *lines.shape[1:])
    own = sum_in_order(pieces, axes, turns)
    whole = gather_in_order(own, axes, turns[::-1]).reshape(-1, *lines.shape[1:])
    return whole[: len(lines)].reshape(x.shape)


def make_amplitudes(k_total, i_energy, j_energy, vir_energy, usable):
    slots = k_total.shape[0]
    orbitals = i_energy.shape[1]
    virtuals = vir_energy.shape[0]
    k_grid = k_total.reshape(slots, orbitals, virtuals, orbitals, virtuals)
    denominator = (
        i_energy[:, :, None, None, None]
        + j_energy[:, None, None, :, None]
        - vir_energy[None, None, :, None, None]
        - vir_energy[None, None, None, None, :]
    )
    values = (2.0 * k_grid - jnp.swapaxes(k_grid, 2, 4)) / denominator
    values = values * usable[:, None, None, None, None]
    return values.astype(jnp.bfloat16).reshape(slots, orbitals * virtuals, orbitals * virtuals)


def local(integrals, occ_count, occ_energy, vir_energy, task_iblock, task_jblock):
    aux_local = integrals.shape[0]
    orbitals = integrals.shape[1]
    virtuals = integrals.shape[2]
    span = orbitals * virtuals
    block_total = lax.axis_size(OROW)
    col_total = lax.axis_size(OCOL)
    my_row = lax.axis_index(OROW)
    my_col = lax.axis_index(OCOL)
    active = jnp.arange(orbitals) < occ_count[my_row]
    masked = integrals * active.astype(jnp.bfloat16)[None, :, None]
    gathered = lax.all_gather(masked, OROW, axis=1, tiled=True)
    flat_blocks = gathered.reshape(aux_local, block_total, span)
    first_list = task_iblock[:, 0]
    task_total = first_list.shape[0]
    per_row = task_total // block_total
    task_ids = my_row * per_row + jnp.arange(per_row)
    i_block = first_list[task_ids]
    j_block = task_jblock[task_ids]
    usable = jnp.ones((per_row,), jnp.float32)
    energy_grid = occ_energy.reshape(block_total, orbitals)
    i_rows = jnp.take(flat_blocks, i_block, axis=1)
    j_rows = jnp.take(flat_blocks, j_block, axis=1)
    k_partial = jnp.einsum("psx,psy->sxy", i_rows, j_rows, preferred_element_type=jnp.float32)
    slots = k_partial.shape[0]
    i_energy = energy_grid[i_block]
    j_energy = energy_grid[j_block]
    k_total = lax.psum(k_partial, OCOL)
    amplitudes = make_amplitudes(k_total, i_energy, j_energy, vir_energy, usable)
    gamma_i = jnp.einsum("sxy,psy->psx", amplitudes, j_rows, preferred_element_type=jnp.float32)
    gamma_j = jnp.einsum("sxy,psx->psy", amplitudes, i_rows, preferred_element_type=jnp.float32)
    slice_width = span // col_total
    amp_grid = amplitudes.reshape(slots, orbitals, virtuals, span)
    column_part = lax.dynamic_slice_in_dim(amp_grid, my_col * slice_width, slice_width, 3)
    dens_part = jnp.einsum(
        "siaw,sibw->ab", column_part, column_part, preferred_element_type=jnp.float32
    )
    block_ids = jnp.arange(block_total)
    i_onehot = (i_block[:, None] == block_ids[None, :]).astype(jnp.float32)
    j_onehot = (j_block[:, None] == block_ids[None, :]).astype(jnp.float32)
    buffer = jnp.einsum(
        "sk,psx->pkx", i_onehot, gamma_i, precision=lax.Precision.HIGHEST
    ) + jnp.einsum("sk,psx->pkx", j_onehot, gamma_j, precision=lax.Precision.HIGHEST)
    owned = lax.psum_scatter(buffer, OROW, scatter_dimension=1, tiled=True)
    gamma_out = owned.reshape(aux_local, orbitals, virtuals)
    density = total_of(dens_part, OROW_OCOL, (0, 1, 2, 3)) / task_total
    return (gamma_out, density)


def solution(mesh):
    finer = Mesh(mesh.devices.reshape(4, 4, 4, 2), ("orow_0", "orow_1", "ocol_0", "ocol_1"))
    placed = (P(OCOL, OROW, None), P(), P(), P(), P(), P())
    return jax.shard_map(
        local, mesh=finer, in_specs=placed, out_specs=(P(OCOL, OROW, None), P()), check_vma=False
    )
```

profile of v0, /device:TPU:1, one launch (start us, length us, event | category | flops | bytes accessed | tf_op | source)
XLA Modules:
  0.0 520.0 jit_solution(48696897312067520)
XLA Ops:
  13.1 66.1 %all-gather.5.cloned.1.call-done = bf16[288,32,384]{2,0,1:T(8,128)(2,1)} async-done(((bf16[288,2,384]{2,0,1:T(8,128)(2,1)}), bf16[288,32,384]{2,0,1:T(8,128)(2,1)}) %all-gather.5.cloned.1.call-update) | async-done | bytes 7077904 | tf_op jit(solution)/shard_map/all_gather | solution.py:74
  79.2 8.5 %copy.47 = bf16[288,32,384]{2,1,0:T(8,128)(2,1)} copy(bf16[288,32,384]{2,0,1:T(8,128)(2,1)} %all-gather.5.cloned.1.call-done) | data formatting | bytes 14155776 | tf_op jit(solution)/shard_map/all_gather | solution.py:74
  87.8 11.3 %reshape.91 = bf16[288,16,768]{2,1,0:T(8,128)(2,1)} reshape(bf16[288,32,384]{2,1,0:T(8,128)(2,1)} %copy.47) | data formatting | bytes 14155776 | tf_op jit(solution)/shard_map/reshape | solution.py:75
  99.1 8.3 %copy.48 = bf16[288,16,768]{2,0,1:T(8,128)(2,1)} copy(bf16[288,16,768]{2,1,0:T(8,128)(2,1)} %reshape.91) | data formatting | bytes 14155776 | tf_op jit(solution)/shard_map/reshape | solution.py:75
  114.8 5.2 fusion.6
  120.0 12.5 %reshape.92 = f32[4,2,384,2,384]{4,3,2,1,0:T(2,128)} reshape(f32[4,768,768]{2,1,0:T(8,128)} %fusion.6) | data formatting | bytes 18874368 | tf_op jit(solution)/shard_map/reshape | solution.py:51
  132.5 14.8 %copy.50 = f32[4,2,384,2,384]{2,4,3,1,0:T(8,128)} copy(f32[4,2,384,2,384]{4,3,2,1,0:T(2,128)} %reshape.92) | data formatting | bytes 18874368 | tf_op jit(solution)/shard_map/reshape | solution.py:51
  157.6 103.2 %all-reduce.9.cloned.1.call-done = f32[4,2,384,2,384]{2,4,3,1,0:T(8,128)} async-done(((f32[4,2,384,2,384]{2,4,3,1,0:T(8,128)}), f32[4,2,384,2,384]{2,4,3,1,0:T(8,128)}) %all-reduce.9.cloned.1.call-update) | async-done | bytes 9437200 | tf_op jit(solution)/shard_map/psum | solution.py:90
  260.8 9.6 %copy.51 = f32[4,2,384,2,384]{4,2,3,1,0:T(8,128)} copy(f32[4,2,384,2,384]{2,4,3,1,0:T(8,128)} %all-reduce.9.cloned.1.call-done) | data formatting | bytes 18874368 | tf_op jit(solution)/shard_map/psum | solution.py:90
  270.4 9.6 %fusion.1 = bf16[4,2,384,2,384]{4,2,3,1,0:T(8,128)(2,1)} fusion(f32[4,2,384,2,384]{2,4,3,1,0:T(8,128)} %all-reduce.9.cloned.1.call-done, f32[4,2,384,2,384]{4,2,3,1,0:T(8,128)} %copy.51, f32[384]{0:T(512)S(1)} %copy-done.2, f32[4,2,384,2]{2,3,1,0:T(2,128)} %broadcast_subtract_fusion), kind=kLoop, calls=%fused_computation.9 | loop fusion | flops 11796480 | bytes 23619072 | tf_op jit(solution)/shard_map/convert_element_type | solution.py:60
  280.0 6.7 %copy.63 = bf16[4,2,384,2,384]{2,4,3,0,1:T(8,128)(2,1)} copy(bf16[4,2,384,2,384]{4,2,3,1,0:T(8,128)(2,1)} %fusion.1) | data formatting | bytes 9437184 | tf_op jit(solution)/shard_map/reshape;reshape | solution.py:95
  286.7 9.4 %copy.52 = bf16[4,2,384,2,384]{4,3,2,1,0:T(2,128)(2,1)} copy(bf16[4,2,384,2,384]{4,2,3,1,0:T(8,128)(2,1)} %fusion.1) | data formatting | bytes 9437184 | tf_op jit(solution)/shard_map/convert_element_type | solution.py:60
  296.1 11.4 %reshape.94 = bf16[4,768,768]{2,1,0:T(8,128)(2,1)} reshape(bf16[4,2,384,2,384]{4,3,2,1,0:T(2,128)(2,1)} %copy.52) | data formatting | bytes 9437184 | tf_op jit(solution)/shard_map/reshape | solution.py:60
  316.5 9.7 %fusion.3 = f32[288,768,16]{1,2,0:T(8,128)} fusion(f32[288,4,768]{2,0,1:T(8,128)S(1)} %convolution_bitcast_fusion.1, s32[4]{0:T(128)S(1)} %copy-done.4), kind=kOutput, calls=%fused_computation.11 | convolution fusion | flops 169869376 | bytes 17694736 | tf_op jit(solution)/shard_map/sk,psx->pkx/dot_general | solution.py:103
  329.5 25.9 %all-reduce.11.cloned.1.call-done = f32[128,3,384]{2,1,0:T(4,128)} async-done(((f32[128,3,384]{2,1,0:T(4,128)}), f32[128,3,384]{2,1,0:T(4,128)}) %all-reduce.11.cloned.1.call-update) | async-done | bytes 589840
  357.1 15.3 %add_bitcast_fusion = f32[288,16,768]{2,1,0:T(8,128)} fusion(f32[288,768,16]{1,2,0:T(8,128)} %fusion.3, f32[288,4,768]{2,0,1:T(8,128)} %convolution_bitcast_fusion, s32[4]{0:T(128)S(1)} %copy-done.6), kind=kOutput, calls=%fused_computation.6 | convolution fusion | flops 173408320 | bytes 31850512 | tf_op jit(solution)/shard_map/sk,psx->pkx/dot_general | solution.py:105
  372.4 18.3 %copy.55 = f32[288,16,768]{2,0,1:T(8,128)} copy(f32[288,16,768]{2,1,0:T(8,128)} %add_bitcast_fusion) | data formatting | bytes 28311552 | tf_op jit(solution)/shard_map/add | solution.py:103
  394.4 5.8 %all-reduce.13.cloned.1.call-done = f32[32,3,384]{2,1,0:T(4,128)} async-done(((f32[32,3,384]{2,1,0:T(4,128)}), f32[32,3,384]{2,1,0:T(4,128)}) %all-reduce.13.cloned.1.call-update) | async-done | bytes 147472
  401.0 14.0 %all-reduce.3 = f32[8,3,384]{2,1,0:T(4,128)S(1)} all-reduce(f32[8,3,384]{2,1,0:T(4,128)S(1)} %constant_dynamic-slice_fusion.1), channel_id=8, replica_groups=mesh['orow_0'=4,'orow_1'=4,'ocol_0'=4,'ocol_1'=2] {'ocol_0'}, use_global_device_ids=true, to_apply=%region_4.6.clone | all-reduce | flops 9216 | bytes 73728
  415.0 9.2 %all-reduce.4 = f32[2,3,384]{2,1,0:T(4,128)S(1)} all-reduce(f32[2,3,384]{2,1,0:T(4,128)S(1)} %constant_dynamic-slice_fusion), channel_id=9, replica_groups=mesh['orow_0'=4,'orow_1'=4,'ocol_0'=4,'ocol_1'=2] {'ocol_1'}, use_global_device_ids=true, to_apply=%region_5.7.clone | all-reduce | flops 2304 | bytes 18432
  426.7 10.1 %all-gather = f32[8,3,384]{2,1,0:T(4,128)S(1)} all-gather(f32[2,3,384]{2,1,0:T(4,128)S(1)} %all_gather.25), channel_id=2, replica_groups=mesh['orow_0'=4,'orow_1'=4,'ocol_0'=4,'ocol_1'=2] {'ocol_0'}, dimensions={0}, use_global_device_ids=true | all-gather | bytes 46080 | tf_op jit(solution)/shard_map/all_gather | solution.py:32
  436.9 11.4 %all-gather.1 = f32[16,2,3,384]{3,1,2,0:T(2,128)S(1)} all-gather(f32[4,2,3,384]{3,1,2,0:T(2,128)S(1)} %copy.58), channel_id=3, replica_groups=mesh['orow_0'=4,'orow_1'=4,'ocol_0'=4,'ocol_1'=2] {'orow_1'}, dimensions={0}, use_global_device_ids=true | all-gather | bytes 184320 | tf_op jit(solution)/shard_map/all_gather | solution.py:32
  448.3 14.9 %all-gather.2 = f32[16,4,2,3,384]{4,1,3,2,0:T(4,128)S(1)} all-gather(f32[4,4,2,3,384]{4,1,3,2,0:T(4,128)S(1)} %copy.59), channel_id=4, replica_groups=mesh['orow_0'=4,'orow_1'=4,'ocol_0'=4,'ocol_1'=2] {'orow_0'}, dimensions={0}, use_global_device_ids=true | all-gather | bytes 737280 | tf_op jit(solution)/shard_map/all_gather | solution.py:32
  464.7 46.0 %reduce-scatter.4.cloned.1.call-done = f32[288,1,768]{2,0,1:T(8,128)} async-done(((f32[288,16,768]{2,0,1:T(8,128)}), f32[288,1,768]{2,0,1:T(8,128)}) %reduce-scatter.4.cloned.1.call-update) | async-done | bytes 884752
  (77 shorter events, 46.6 us)
Async XLA Ops:
  7.2 4.0 copy-start
  7.2 72.1 %all-gather.5.cloned.1.call-start = ((), (), s32[]{:S(2)}) async-start(), calls=%async_computation.1 | async-start | bytes 7520256 | tf_op jit(solution)/shard_map/all_gather | solution.py:74
  11.0 249.8 %all-reduce.9.cloned.1.call-start = ((), (), s32[]{:S(2)}) async-start(), calls=%async_computation.2 | async-start | bytes 18874368 | tf_op jit(solution)/shard_map/psum | solution.py:90
  11.8 76.0 %copy-start.3 = (s32[4]{0:T(128)}, s32[4]{0:T(128)S(1)}, u32[]{:S(2)}) copy-start(s32[4]{0:T(128)S(1)} %gather_fusion.1) | copy-start | bytes 52
  13.1 74.7 %copy-start.5 = (s32[4]{0:T(128)}, s32[4]{0:T(128)S(1)}, u32[]{:S(2)}) copy-start(s32[4]{0:T(128)S(1)} %gather_fusion) | copy-start | bytes 52
  147.3 208.0 %all-reduce.11.cloned.1.call-start = ((), (), s32[]{:S(2)}) async-start(), calls=%async_computation.3 | async-start | bytes 1572864
  157.6 112.8 %copy-start.2 = (f32[384]{0:T(512)S(1)}, f32[384]{0:T(512)}, u32[]{:S(2)}) copy-start(f32[384]{0:T(512)} %param.11) | copy-start | bytes 4612
  312.3 4.2 copy-start.4
  312.3 87.9 %all-reduce.13.cloned.1.call-start = ((), (), s32[]{:S(2)}) async-start(), calls=%async_computation.4 | async-start | bytes 393216
  312.5 13.7 %slice-start = ((s8[4718592]{0:T(1024)(128)(4,1)}), s8[524288]{0:T(1024)(128)(4,1)S(1)}, s32[]{:S(2)}) async-start(s8[4718592]{0:T(1024)(128)(4,1)} %bitcast.58), calls=%async_computation.6 | async-start | bytes 1048576
  316.5 9.7 %slice-start.1 = ((s8[4718592]{0:T(1024)(128)(4,1)}), s8[4194304]{0:T(1024)(128)(4,1)S(1)}, s32[]{:S(2)}) async-start(s8[4718592]{0:T(1024)(128)(4,1)} %bitcast.58), calls=%async_computation.7 | async-start | bytes 8388608
  326.2 30.9 %copy-start.6 = (s32[4]{0:T(128)S(1)}, s32[4]{0:T(128)}, u32[]{:S(2)}) copy-start(s32[4]{0:T(128)} %copy-done.5) | copy-start | bytes 52
  357.0 153.6 %reduce-scatter.4.cloned.1.call-start = ((), (), s32[]{:S(2)}) async-start(), calls=%async_computation.5 | async-start | bytes 15040512
  390.7 0.7 copy-start.9
  390.7 1.2 copy-start.8
  390.7 1.9 copy-start.7
  391.3 121.9 %copy-start.1 = (s32[64,1]{0,1:T(1,128)S(1)}, s32[64,1]{0,1:T(1,128)}, u32[]{:S(2)}) copy-start(s32[64,1]{0,1:T(1,128)} %param.12) | copy-start | bytes 772
Sparse Core Ops, SparseCore 0:
  11.2 68.0 all-gather.4
  147.5 113.3 all-reduce.8
  312.4 42.9 all-reduce.10
  358.1 42.0 all-reduce.12
  403.6 107.0 reduce-scatter.3
where the time goes:
time: 529 us; the launch traced here: 520 us
  waiting for transfers between devices  247 us (47%)
  local copies, waits for them, and re-layouts  138 us (26%)
  blocking collectives  61.5 us (12%)
  matrix products  40 us (8%)
  other arithmetic  16.9 us (3%)
  between operations  16.2 us (3%)
    psum x1, waiting for transfers between devices, local(): k_total = lax.psum(k_partial, OCOL)  103 us
    unnamed x8, waiting for transfers between devices  77.7 us
    all_gather x1, waiting for transfers between devices, local(): gathered = lax.all_gather(masked, OROW, axis=1, tiled=True)  66.1 us
    all_gather x4, blocking collectives, gather_in_order(): pieces = lax.all_gather(pieces, axes[k])  38.2 us
    reshape x2, local copies, waits for them, and re-layouts, make_amplitudes(): k_grid = k_total.reshape(slots, orbitals, virtuals, orbitals, virtuals)  27.3 us
    unnamed x2, blocking collectives  23.3 us
    reshape x2, local copies, waits for them, and re-layouts, local(): flat_blocks = gathered.reshape(aux_local, block_total, span)  19.6 us
    add x1, local copies, waits for them, and re-layouts, local(): jnp.einsum('sk,psx->pkx', i_onehot, gamma_i, precision=lax.Precision.HIGH...  18.3 us
  transfers between devices with their start and end apart: 5, of which 5 were waited for; matrix products, arithmetic and copies ran while one was open for 13% of the time, Pallas kernels for 0%

commit v1 on v0

--- a/solution.py
+++ b/solution.py
@@ -71,7 +71,7 @@
     my_col = lax.axis_index(OCOL)
     active = jnp.arange(orbitals) < occ_count[my_row]
     masked = integrals * active.astype(jnp.bfloat16)[None, :, None]
-    gathered = lax.all_gather(masked, OROW, axis=1, tiled=True)
+    gathered = jnp.concatenate(lax.all_gather(masked, OROW), axis=1)
     flat_blocks = gathered.reshape(aux_local, block_total, span)
     first_list = task_iblock[:, 0]
     task_total = first_list.shape[0]

time: 529 us -> 510 us (0.964); the launches traced: 520 us -> 508 us
  local copies, waits for them, and re-layouts: 138 us -> 126 us
    reshape x2 -> x0, local copies, waits for them, and re-layouts: 19.6 us -> none  [local(): flat_blocks = gathered.reshape(aux_local, block_total, span)]
    another operation x0 -> x1, local copies, waits for them, and re-layouts: none -> 16.1 us  [local(): flat_blocks = gathered.reshape(aux_local, block_total, span)]
    all_gather x1 -> x0, local copies, waits for them, and re-layouts: 8.54 us -> none  [local(): gathered = lax.all_gather(masked, OROW, axis=1, tiled=True)]
where the time goes in v1:
time: 510 us; the launch traced here: 508 us
  waiting for transfers between devices  248 us (49%)
  local copies, waits for them, and re-layouts  126 us (25%)
  blocking collectives  61.5 us (12%)
  matrix products  39.8 us (8%)
  other arithmetic  17.2 us (3%)
  between operations  15.9 us (3%)
    psum x1, waiting for transfers between devices, local(): k_total = lax.psum(k_partial, OCOL)  103 us
    unnamed x8, waiting for transfers between devices  78.2 us
    all_gather x1, waiting for transfers between devices, local(): gathered = jnp.concatenate(lax.all_gather(masked, OROW), axis=1)  66.1 us
    all_gather x4, blocking collectives, gather_in_order(): pieces = lax.all_gather(pieces, axes[k])  38.2 us
    reshape x2, local copies, waits for them, and re-layouts, make_amplitudes(): k_grid = k_total.reshape(slots, orbitals, virtuals, orbitals, virtuals)  27.3 us
    unnamed x2, blocking collectives  23.3 us
    add x1, local copies, waits for them, and re-layouts, local(): jnp.einsum('sk,psx->pkx', i_onehot, gamma_i, precision=lax.Precision.HIGH...  18.3 us
    another operation x1, local copies, waits for them, and re-layouts, local(): flat_blocks = gathered.reshape(aux_local, block_total, span)  16.1 us
  transfers between devices with their start and end apart: 5, of which 5 were waited for; matrix products, arithmetic and copies ran while one was open for 13% of the time, Pallas kernels for 0%

profile of v1, /device:TPU:1, one launch (start us, length us, event | category | flops | bytes accessed | tf_op | source)
XLA Modules:
  0.0 508.3 jit_solution(3432564666053384925)
XLA Ops:
  13.5 66.1 %all-gather.6.cloned.1.call-done = bf16[4608,2,384]{2,1,0:T(2,128)(2,1)} async-done(((bf16[288,2,384]{2,1,0:T(2,128)(2,1)}), bf16[4608,2,384]{2,1,0:T(2,128)(2,1)}) %all-gather.6.cloned.1.call-update) | async-done | bytes 7077904 | tf_op jit(solution)/shard_map/all_gather | solution.py:74
  79.6 16.1 %reshape_reshape.7 = bf16[288,16,768]{2,0,1:T(8,128)(2,1)} reshape(bf16[288,16,2,384]{3,2,0,1:T(2,128)(2,1)} %bitcast.65) | data formatting | bytes 14155776 | tf_op jit(solution)/shard_map/reshape;reshape | solution.py:75
  99.4 3.7 gather_fusion.4
  103.0 5.2 %fusion.6 = f32[4,768,768]{2,1,0:T(8,128)} fusion(bf16[4,288,768]{2,1,0:T(8,128)(2,1)S(1)} %gather_fusion.4, pred[4]{0:T(512)(128)(4,1)S(1)} %get-tuple-element.4, bf16[4,288,768]{2,1,0:T(8,128)(2,1)S(1)} %gather_fusion.5, pred[4]{0:T(512)(128)(4,1)S(1)} %get-tuple-element.3), kind=kOutput, calls=%fused_computation.16 | convolution fusion | flops 1360723968 | bytes 12976136 | tf_op jit(solution)/shard_map/psx,psy->sxy/dot_general | solution.py:86
  108.2 12.5 %reshape.92 = f32[4,2,384,2,384]{4,3,2,1,0:T(2,128)} reshape(f32[4,768,768]{2,1,0:T(8,128)} %fusion.6) | data formatting | bytes 18874368 | tf_op jit(solution)/shard_map/reshape | solution.py:51
  120.8 14.8 %copy.31 = f32[4,2,384,2,384]{2,4,3,1,0:T(8,128)} copy(f32[4,2,384,2,384]{4,3,2,1,0:T(2,128)} %reshape.92) | data formatting | bytes 18874368 | tf_op jit(solution)/shard_map/reshape | solution.py:51
  145.6 103.5 %all-reduce.9.cloned.1.call-done = f32[4,2,384,2,384]{2,4,3,1,0:T(8,128)} async-done(((f32[4,2,384,2,384]{2,4,3,1,0:T(8,128)}), f32[4,2,384,2,384]{2,4,3,1,0:T(8,128)}) %all-reduce.9.cloned.1.call-update) | async-done | bytes 9437200 | tf_op jit(solution)/shard_map/psum | solution.py:90
  249.1 9.6 %copy.32 = f32[4,2,384,2,384]{4,2,3,1,0:T(8,128)} copy(f32[4,2,384,2,384]{2,4,3,1,0:T(8,128)} %all-reduce.9.cloned.1.call-done) | data formatting | bytes 18874368 | tf_op jit(solution)/shard_map/psum | solution.py:90
  258.7 9.6 %fusion.1 = bf16[4,2,384,2,384]{4,2,3,1,0:T(8,128)(2,1)} fusion(f32[4,2,384,2,384]{2,4,3,1,0:T(8,128)} %all-reduce.9.cloned.1.call-done, f32[4,2,384,2,384]{4,2,3,1,0:T(8,128)} %copy.32, f32[384]{0:T(512)S(1)} %copy-done.2, f32[4,2,384,2]{2,3,1,0:T(2,128)} %broadcast_subtract_fusion), kind=kLoop, calls=%fused_computation.9 | loop fusion | flops 11796480 | bytes 23619072 | tf_op jit(solution)/shard_map/convert_element_type | solution.py:60
  268.2 6.7 %copy.44 = bf16[4,2,384,2,384]{2,4,3,0,1:T(8,128)(2,1)} copy(bf16[4,2,384,2,384]{4,2,3,1,0:T(8,128)(2,1)} %fusion.1) | data formatting | bytes 9437184 | tf_op jit(solution)/shard_map/reshape;reshape | solution.py:95
  274.9 9.4 %copy.33 = bf16[4,2,384,2,384]{4,3,2,1,0:T(2,128)(2,1)} copy(bf16[4,2,384,2,384]{4,2,3,1,0:T(8,128)(2,1)} %fusion.1) | data formatting | bytes 9437184 | tf_op jit(solution)/shard_map/convert_element_type | solution.py:60
  284.4 11.4 %reshape.94 = bf16[4,768,768]{2,1,0:T(8,128)(2,1)} reshape(bf16[4,2,384,2,384]{4,3,2,1,0:T(2,128)(2,1)} %copy.33) | data formatting | bytes 9437184 | tf_op jit(solution)/shard_map/reshape | solution.py:60
  300.8 4.0 convolution_bitcast_fusion.1
  304.8 9.7 %fusion.3 = f32[288,768,16]{1,2,0:T(8,128)} fusion(f32[288,4,768]{2,0,1:T(8,128)S(1)} %convolution_bitcast_fusion.1, s32[4]{0:T(128)S(1)} %copy-done.4), kind=kOutput, calls=%fused_computation.11 | convolution fusion | flops 169869376 | bytes 17694736 | tf_op jit(solution)/shard_map/sk,psx->pkx/dot_general | solution.py:103
  317.8 25.8 %all-reduce.11.cloned.1.call-done = f32[128,3,384]{2,1,0:T(4,128)} async-done(((f32[128,3,384]{2,1,0:T(4,128)}), f32[128,3,384]{2,1,0:T(4,128)}) %all-reduce.11.cloned.1.call-update) | async-done | bytes 589840
  345.4 15.1 %add_bitcast_fusion = f32[288,16,768]{2,1,0:T(8,128)} fusion(f32[288,768,16]{1,2,0:T(8,128)} %fusion.3, f32[288,4,768]{2,0,1:T(8,128)} %convolution_bitcast_fusion, s32[4]{0:T(128)S(1)} %copy-done.6), kind=kOutput, calls=%fused_computation.6 | convolution fusion | flops 173408320 | bytes 31850512 | tf_op jit(solution)/shard_map/sk,psx->pkx/dot_general | solution.py:105
  360.4 18.3 %copy.36 = f32[288,16,768]{2,0,1:T(8,128)} copy(f32[288,16,768]{2,1,0:T(8,128)} %add_bitcast_fusion) | data formatting | bytes 28311552 | tf_op jit(solution)/shard_map/add | solution.py:103
  382.5 6.0 %all-reduce.13.cloned.1.call-done = f32[32,3,384]{2,1,0:T(4,128)} async-done(((f32[32,3,384]{2,1,0:T(4,128)}), f32[32,3,384]{2,1,0:T(4,128)}) %all-reduce.13.cloned.1.call-update) | async-done | bytes 147472
  389.3 14.0 %all-reduce.3 = f32[8,3,384]{2,1,0:T(4,128)S(1)} all-reduce(f32[8,3,384]{2,1,0:T(4,128)S(1)} %constant_dynamic-slice_fusion.1), channel_id=9, replica_groups=mesh['orow_0'=4,'orow_1'=4,'ocol_0'=4,'ocol_1'=2] {'ocol_0'}, use_global_device_ids=true, to_apply=%region_4.6.clone | all-reduce | flops 9216 | bytes 73728
  403.3 9.2 %all-reduce.4 = f32[2,3,384]{2,1,0:T(4,128)S(1)} all-reduce(f32[2,3,384]{2,1,0:T(4,128)S(1)} %constant_dynamic-slice_fusion), channel_id=10, replica_groups=mesh['orow_0'=4,'orow_1'=4,'ocol_0'=4,'ocol_1'=2] {'ocol_1'}, use_global_device_ids=true, to_apply=%region_5.7.clone | all-reduce | flops 2304 | bytes 18432
  415.0 10.1 %all-gather.1 = f32[8,3,384]{2,1,0:T(4,128)S(1)} all-gather(f32[2,3,384]{2,1,0:T(4,128)S(1)} %all_gather.29), channel_id=3, replica_groups=mesh['orow_0'=4,'orow_1'=4,'ocol_0'=4,'ocol_1'=2] {'ocol_0'}, dimensions={0}, use_global_device_ids=true | all-gather | bytes 46080 | tf_op jit(solution)/shard_map/all_gather | solution.py:32
  425.1 11.3 %all-gather.2 = f32[16,2,3,384]{3,1,2,0:T(2,128)S(1)} all-gather(f32[4,2,3,384]{3,1,2,0:T(2,128)S(1)} %copy.39), channel_id=4, replica_groups=mesh['orow_0'=4,'orow_1'=4,'ocol_0'=4,'ocol_1'=2] {'orow_1'}, dimensions={0}, use_global_device_ids=true | all-gather | bytes 184320 | tf_op jit(solution)/shard_map/all_gather | solution.py:32
  436.5 14.9 %all-gather.3 = f32[16,4,2,3,384]{4,1,3,2,0:T(4,128)S(1)} all-gather(f32[4,4,2,3,384]{4,1,3,2,0:T(4,128)S(1)} %copy.40), channel_id=5, replica_groups=mesh['orow_0'=4,'orow_1'=4,'ocol_0'=4,'ocol_1'=2] {'orow_0'}, dimensions={0}, use_global_device_ids=true | all-gather | bytes 737280 | tf_op jit(solution)/shard_map/all_gather | solution.py:32
  453.0 46.2 %reduce-scatter.4.cloned.1.call-done = f32[288,1,768]{2,0,1:T(8,128)} async-done(((f32[288,16,768]{2,0,1:T(8,128)}), f32[288,1,768]{2,0,1:T(8,128)}) %reduce-scatter.4.cloned.1.call-update) | async-done | bytes 884752
  (75 shorter events, 39.1 us)
Async XLA Ops:
  7.2 4.3 copy-start
  7.2 72.4 %all-gather.6.cloned.1.call-start = ((), (), s32[]{:S(2)}) async-start(), calls=%async_computation.2 | async-start | bytes 7520256 | tf_op jit(solution)/shard_map/all_gather | solution.py:74
  11.4 237.7 %all-reduce.9.cloned.1.call-start = ((), (), s32[]{:S(2)}) async-start(), calls=%async_computation.1 | async-start | bytes 18874368 | tf_op jit(solution)/shard_map/psum | solution.py:90
  12.1 83.6 %copy-start.3 = (s32[4]{0:T(128)}, s32[4]{0:T(128)S(1)}, u32[]{:S(2)}) copy-start(s32[4]{0:T(128)S(1)} %gather_fusion.1) | copy-start | bytes 52
  13.4 82.3 %copy-start.5 = (s32[4]{0:T(128)}, s32[4]{0:T(128)S(1)}, u32[]{:S(2)}) copy-start(s32[4]{0:T(128)S(1)} %gather_fusion) | copy-start | bytes 52
  135.6 208.1 %all-reduce.11.cloned.1.call-start = ((), (), s32[]{:S(2)}) async-start(), calls=%async_computation.3 | async-start | bytes 1572864
  145.6 113.1 %copy-start.2 = (f32[384]{0:T(512)S(1)}, f32[384]{0:T(512)}, u32[]{:S(2)}) copy-start(f32[384]{0:T(512)} %param.11) | copy-start | bytes 4612
  300.5 4.3 copy-start.4
  300.5 88.0 %all-reduce.13.cloned.1.call-start = ((), (), s32[]{:S(2)}) async-start(), calls=%async_computation.4 | async-start | bytes 393216
  300.8 13.7 %slice-start = ((s8[4718592]{0:T(1024)(128)(4,1)}), s8[524288]{0:T(1024)(128)(4,1)S(1)}, s32[]{:S(2)}) async-start(s8[4718592]{0:T(1024)(128)(4,1)} %bitcast.63), calls=%async_computation.6 | async-start | bytes 1048576
  304.8 9.7 %slice-start.1 = ((s8[4718592]{0:T(1024)(128)(4,1)}), s8[4194304]{0:T(1024)(128)(4,1)S(1)}, s32[]{:S(2)}) async-start(s8[4718592]{0:T(1024)(128)(4,1)} %bitcast.63), calls=%async_computation.7 | async-start | bytes 8388608
  314.5 30.9 %copy-start.6 = (s32[4]{0:T(128)S(1)}, s32[4]{0:T(128)}, u32[]{:S(2)}) copy-start(s32[4]{0:T(128)} %copy-done.5) | copy-start | bytes 52
  345.3 153.9 %reduce-scatter.4.cloned.1.call-start = ((), (), s32[]{:S(2)}) async-start(), calls=%async_computation.5 | async-start | bytes 15040512
  378.8 0.7 copy-start.9
  378.8 1.2 copy-start.8
  378.8 1.9 copy-start.7
  413.2 88.6 %copy-start.1 = (s32[64,1]{0,1:T(1,128)S(1)}, s32[64,1]{0,1:T(1,128)}, u32[]{:S(2)}) copy-start(s32[64,1]{0,1:T(1,128)} %param.12) | copy-start | bytes 772
Sparse Core Ops, SparseCore 0:
  11.5 68.0 all-gather.5
  135.7 113.3 all-reduce.8
  300.6 42.9 all-reduce.10
  346.4 42.0 all-reduce.12
  391.8 107.3 reduce-scatter.3
